TPU v7x, 256 devices: a whole 4x4x8 slice. The times are simulated.
256 devices in a mesh: member: 16 (over z_lo, x), grid: 16 (over z_hi, y, core).
Axes of the slice: x: 4, y: 4, z: 8 (z_hi: 2, z_lo: 4; z = z_hi * 4 + z_lo), core: 2. Of those that a mesh axis runs over, the one named last changes fastest.
Arguments:
- slabs: bfloat16 [16, 4096, 256], P('member', 'grid'), may hold values from -6 to 6
- loader: int32 [1], replicated, may hold values from 0 to 15
- hidden_jitter: bfloat16 [16, 2048, 16], P('member', 'grid'), may hold values from -3 to 3
- w_noise: bfloat16 [16, 1024], replicated, may hold values from -1.5 to 1.5
- w_enc: bfloat16 [128, 1024], replicated, may hold values from -0.10986328 to 0.10986328
- enc_offset: int32 [2048, 8], P('grid'), may hold values from -128 to 128
- enc_weight: float32 [2048, 8], P('grid'), may hold values from -1 to 1
- w_qkv: bfloat16 [1024, 1536], replicated, may hold values from -0.1875 to 0.1875
- window_offset: int32 [2048], P('grid'), may hold values from -64 to 0
- w_out: bfloat16 [512, 1024], replicated, may hold values from -0.25 to 0.25
- unpacker_linear_map: bfloat16 [1024, 128], replicated, may hold values from -0.1875 to 0.1875
- dec_offset: int32 [4096, 3], P('grid'), may hold values from -64 to 64
- unpacker_arc_scales: float32 [4096, 3], P('grid'), may hold values from 0.2 to 1
Outputs:
- grad_noise: float32 [16, 1024], P(None, ('member', 'grid'))
- grad_enc: float32 [128, 1024], P(None, ('member', 'grid'))
- grad_qkv: float32 [1024, 1536], P(('member', 'grid'))
- grad_out: float32 [512, 1024], P(None, ('member', 'grid'))
- unpacker_map_sensitivity: float32 [1024, 128], P(('member', 'grid'))
All inputs are finite; a program needn't handle non-finite values.
Results may differ from a plain program's by a relative error of at most 0.0075.
Values may be sent and summed in bfloat16 or wider, within the bound.
No kernel may reach another device: no remote copies, remote signals or barrier semaphores. Data moves between devices by JAX's collectives and lax.ppermute only.
A program may use at most 128 MiB of HBM per device.

v0:
```python
import jax
import jax.numpy as jnp
from jax import lax
from jax.sharding import PartitionSpec as P

HEAD_DIM = 64
RIM_G = 128
RIM_H = 64
WIN = 64
EPS = 1e-06
DELTA_SQ = 0.01


def extended(block, sides, width):
    for axis, dim in sides:
        count = lax.axis_size(axis)
        forward = [(i, i + 1) for i in range(count - 1)]
        forward.append((count - 1, 0))
        backward = [(target, source) for source, target in forward]
        low = lax.ppermute(
            lax.slice_in_dim(block, block.shape[dim] - width, None, axis=dim), axis, forward
        )
        high = lax.ppermute(lax.slice_in_dim(block, 0, width, axis=dim), axis, backward)
        block = jnp.concatenate([low, block, high], axis=dim)
    return block


def broadcast(x, axis, root):
    mine = lax.axis_index(axis) == root
    return lax.psum(jnp.where(mine, x, jnp.zeros_like(x)), axis)


def rms_factor(values):
    return lax.rsqrt(jnp.mean(values * values, axis=-1, keepdims=True) + EPS)


def rms_back(values, factor, gradient):
    inner = jnp.mean(gradient * values, axis=-1, keepdims=True)
    return factor * gradient - values * (factor * factor * factor) * inner


def silu_slope(pre):
    sigma = jax.nn.sigmoid(pre)
    return sigma * (1.0 + pre * (1.0 - sigma))


def eased_sensitivity(diff):
    return diff * lax.rsqrt(diff * diff + DELTA_SQ)


def plain_rims(values, depth):
    return extended(values, (("grid", 0),), depth)


def exact_rims(values, depth):
    return extended(values.astype(jnp.bfloat16), (("grid", 0),), depth).astype(values.dtype)


def fold_back(grad_ext, depth):
    edges = jnp.concatenate([grad_ext[:depth], grad_ext[-depth:]], axis=0)
    beside_all = exact_rims(edges, depth)
    inner_rows = grad_ext[depth:-depth]
    inner_rows = inner_rows.at[:depth].add(beside_all[:depth])
    return inner_rows.at[-depth:].add(beside_all[-depth:])


def realization_rotate(values):
    return lax.all_to_all(
        values.astype(jnp.bfloat16), "member", split_axis=0, concat_axis=0, tiled=True
    ).astype(values.dtype)


def rows_product(left, right):
    return lax.dot_general(
        left, right, (((0,), (0,)), ((), ())), preferred_element_type=jnp.float32
    )


def faithful_cells(left, right):
    return lax.dot_general(left, right, (((0,), (0,)), ((), ())), precision=lax.Precision.HIGHEST)


def cols_product(left, right):
    return lax.dot_general(
        left, right, (((1,), (1,)), ((), ())), preferred_element_type=jnp.float32
    )


def faithful_widths(left, right):
    return lax.dot_general(left, right, (((1,), (1,)), ((), ())), precision=lax.Precision.HIGHEST)


def per_device(
    slabs,
    loader,
    hidden_jitter,
    w_noise,
    w_enc,
    enc_offset,
    enc_weight,
    w_qkv,
    window_offset,
    w_out,
    unpacker_linear_map,
    dec_offset,
    unpacker_arc_scales,
):
    realization_array = lax.axis_size("member")
    shards = lax.axis_size("grid")
    analysis = broadcast(slabs[0], "member", loader[0])
    variable_tally = w_enc.shape[0]
    model_width = w_enc.shape[1]
    attn_width = w_out.shape[0]
    head_count = attn_width // HEAD_DIM
    lattice_cell_amounts = analysis.shape[0]
    node_rows = enc_offset.shape[0]
    inv_root = HEAD_DIM ** (-0.5)
    unadorned_state = analysis[:, :variable_tally]
    verifying_cell_amounts = analysis[:, variable_tally:]
    x_ext = plain_rims(unadorned_state, RIM_G)
    pre_enc = jnp.dot(x_ext, w_enc, preferred_element_type=jnp.float32)
    messages = jax.nn.silu(pre_enc).astype(jnp.bfloat16)
    home_rows = jnp.arange(node_rows, dtype=jnp.int32) * lattice_cell_amounts // node_rows
    enc_source = home_rows[:, None] + enc_offset + RIM_G
    averaged_cells = jnp.zeros((node_rows, model_width), jnp.float32)
    for arc_location in range(enc_offset.shape[1]):
        averaged_cells = averaged_cells + enc_weight[:, arc_location : arc_location + 1] * messages[
            enc_source[:, arc_location]
        ].astype(jnp.float32)
    factor0 = rms_factor(averaged_cells)
    jitter_cell_amounts = hidden_jitter[0]
    state0 = averaged_cells * factor0 + jnp.dot(
        jitter_cell_amounts, w_noise, preferred_element_type=jnp.float32
    )
    factor1 = rms_factor(state0)
    normed = (state0 * factor1).astype(jnp.bfloat16)
    mixed_rows = jnp.dot(normed, w_qkv, preferred_element_type=jnp.float32).reshape(
        node_rows, 3, head_count, HEAD_DIM
    )
    queries = mixed_rows[:, 0]
    key_raw = mixed_rows[:, 1]
    query_factor = rms_factor(queries)
    key_factor = rms_factor(key_raw)
    query_norm = (queries * query_factor).astype(jnp.bfloat16)
    key_norm = (key_raw * key_factor).astype(jnp.bfloat16)
    value_rows = mixed_rows[:, 2].astype(jnp.bfloat16)
    packed = jnp.concatenate(
        [key_norm.reshape(node_rows, attn_width), value_rows.reshape(node_rows, attn_width)], axis=1
    )
    packed_ext = plain_rims(packed, WIN)
    key_ext = packed_ext[:, :attn_width].reshape(-1, head_count, HEAD_DIM)
    value_ext = packed_ext[:, attn_width:].reshape(-1, head_count, HEAD_DIM)
    span_rows = node_rows + 2 * WIN
    relative = (
        jnp.arange(span_rows, dtype=jnp.int32)[None, :]
        - WIN
        - jnp.arange(node_rows, dtype=jnp.int32)[:, None]
    )
    starts = list(range(0, node_rows, node_rows))
    prob_blocks = []
    out_blocks = []
    for first_row in starts:
        query_block = query_norm
        key_block = key_ext
        value_block = value_ext
        offsets = window_offset[first_row : first_row + node_rows, None]
        allowed = ((relative >= offsets) & (relative < offsets + WIN)).astype(jnp.float32)
        scores = (
            jnp.einsum("qhd,khd->hqk", query_block, key_block, preferred_element_type=jnp.float32)
            * inv_root
        )
        weights_exp = jnp.exp(scores) * allowed[None]
        prob_block = (weights_exp / jnp.sum(weights_exp, axis=-1, keepdims=True)).astype(
            jnp.bfloat16
        )
        prob_blocks.append(prob_block)
        out_blocks.append(
            jnp.einsum(
                "hqk,khd->qhd", prob_block, value_block, preferred_element_type=jnp.float32
            ).astype(jnp.bfloat16)
        )
    attended = out_blocks[0].reshape(node_rows, attn_width)
    state1 = state0 + jnp.dot(attended, w_out, preferred_element_type=jnp.float32)
    factor2 = rms_factor(state1)
    dnorm = (state1 * factor2).astype(jnp.bfloat16)
    home_nodes = (
        jnp.arange(lattice_cell_amounts, dtype=jnp.int32) * node_rows // lattice_cell_amounts
    )
    unpacker_start_cell = home_nodes[:, None] + dec_offset + RIM_H
    dnorm_ext = plain_rims(dnorm, RIM_H)
    assembled_cells = jnp.zeros((lattice_cell_amounts, model_width), jnp.float32)
    for arc_location in range(dec_offset.shape[1]):
        assembled_cells = assembled_cells + unpacker_arc_scales[
            :, arc_location : arc_location + 1
        ] * dnorm_ext[unpacker_start_cell[:, arc_location]].astype(jnp.float32)
    restored_cells = jnp.dot(
        assembled_cells, unpacker_linear_map.astype(jnp.float32), precision=lax.Precision.HIGHEST
    )
    prognosis_cells = unadorned_state.astype(jnp.float32) + restored_cells
    subset_cells = lattice_cell_amounts // realization_array
    realization_cells = realization_rotate(
        prognosis_cells.reshape(realization_array, subset_cells, variable_tally)
    )
    member_index = lax.axis_index("member")
    truth_block = lax.dynamic_slice_in_dim(
        verifying_cell_amounts, member_index * subset_cells, subset_cells, 0
    ).astype(jnp.float32)
    loss_scale = float(realization_array * lattice_cell_amounts * shards * variable_tally) ** (-0.5)
    verifying_sensitivity = eased_sensitivity(realization_cells - truth_block[None])
    duo_spread_sum = jnp.sum(
        eased_sensitivity(realization_cells[:, None] - realization_cells[None, :]), axis=1
    )
    realization_sensitivity_array = (
        verifying_sensitivity / realization_array
        - duo_spread_sum / (realization_array * (realization_array - 1))
    ) * loss_scale
    prognosis_sensitivity = realization_rotate(realization_sensitivity_array).reshape(
        lattice_cell_amounts, variable_tally
    )
    assembled_sensitivity = faithful_widths(
        prognosis_sensitivity, unpacker_linear_map.astype(jnp.float32)
    )
    unpacker_map_sensitivity = faithful_cells(assembled_cells, prognosis_sensitivity)
    grad_dnorm_ext = jnp.zeros(dnorm_ext.shape, jnp.float32)
    for arc_location in range(dec_offset.shape[1]):
        grad_dnorm_ext = grad_dnorm_ext.at[unpacker_start_cell[:, arc_location]].add(
            unpacker_arc_scales[:, arc_location : arc_location + 1] * assembled_sensitivity
        )
    grad_dnorm = fold_back(grad_dnorm_ext, RIM_H)
    grad_state1 = rms_back(state1, factor2, grad_dnorm)
    grad_state1_b = grad_state1.astype(jnp.bfloat16)
    grad_out = rows_product(attended, grad_state1_b)
    grad_attended = (
        cols_product(grad_state1_b, w_out)
        .astype(jnp.bfloat16)
        .reshape(node_rows, head_count, HEAD_DIM)
    )
    grad_packed_ext = jnp.zeros((node_rows + 2 * WIN, 2 * attn_width), jnp.float32)
    grad_query_blocks = []
    for block_index, first_row in enumerate(starts):
        query_block = query_norm
        key_block = key_ext
        value_block = value_ext
        prob_block = prob_blocks[block_index]
        grad_probs = jnp.einsum(
            "qhd,khd->hqk", grad_attended, value_block, preferred_element_type=jnp.float32
        )
        prob_wide = prob_block.astype(jnp.float32)
        grad_scores = (
            prob_wide * (grad_probs - jnp.sum(prob_wide * grad_probs, axis=-1, keepdims=True))
        ).astype(jnp.bfloat16)
        grad_query_blocks.append(
            jnp.einsum("hqk,khd->qhd", grad_scores, key_block, preferred_element_type=jnp.float32)
            * inv_root
        )
        grad_key_block = (
            jnp.einsum("hqk,qhd->khd", grad_scores, query_block, preferred_element_type=jnp.float32)
            * inv_root
        )
        grad_value_block = jnp.einsum(
            "hqk,qhd->khd", prob_block, grad_attended, preferred_element_type=jnp.float32
        )
        grad_pair = jnp.concatenate(
            [
                grad_key_block.reshape(span_rows, attn_width),
                grad_value_block.reshape(span_rows, attn_width),
            ],
            axis=1,
        )
        grad_packed_ext = grad_packed_ext.at[first_row : first_row + span_rows].add(grad_pair)
    grad_packed = fold_back(grad_packed_ext, WIN)
    grad_knorm = grad_packed[:, :attn_width].reshape(node_rows, head_count, HEAD_DIM)
    grad_values = grad_packed[:, attn_width:].reshape(node_rows, head_count, HEAD_DIM)
    grad_qnorm = grad_query_blocks[0]
    grad_queries = rms_back(queries, query_factor, grad_qnorm)
    grad_keys = rms_back(key_raw, key_factor, grad_knorm)
    grad_mixed = (
        jnp.stack([grad_queries, grad_keys, grad_values], axis=1)
        .reshape(node_rows, 3 * attn_width)
        .astype(jnp.bfloat16)
    )
    grad_qkv = rows_product(normed, grad_mixed)
    grad_normed = cols_product(grad_mixed, w_qkv)
    grad_state0 = grad_state1 + rms_back(state0, factor1, grad_normed)
    grad_noise = rows_product(jitter_cell_amounts, grad_state0.astype(jnp.bfloat16))
    grad_pooled = rms_back(averaged_cells, factor0, grad_state0)
    grad_messages = jnp.zeros((x_ext.shape[0], model_width), jnp.float32)
    for arc_location in range(enc_offset.shape[1]):
        grad_messages = grad_messages.at[enc_source[:, arc_location]].add(
            enc_weight[:, arc_location : arc_location + 1] * grad_pooled
        )
    grad_enc = faithful_cells(x_ext.astype(jnp.float32), grad_messages * silu_slope(pre_enc))
    grad_noise, grad_enc, grad_qkv, grad_out, unpacker_map_sensitivity = (
        lax.psum_scatter(grad_noise, ("member", "grid"), scatter_dimension=1, tiled=True),
        lax.psum_scatter(grad_enc, ("member", "grid"), scatter_dimension=1, tiled=True),
        lax.psum_scatter(grad_qkv, ("member", "grid"), scatter_dimension=0, tiled=True),
        lax.psum_scatter(grad_out, ("member", "grid"), scatter_dimension=1, tiled=True),
        lax.psum_scatter(
            unpacker_map_sensitivity, ("member", "grid"), scatter_dimension=0, tiled=True
        ),
    )
    return (grad_noise, grad_enc, grad_qkv, grad_out, unpacker_map_sensitivity)


def solution(mesh):
    in_specs = (
        P("member", "grid", None),
        P(),
        P("member", "grid", None),
        P(),
        P(),
        P("grid", None),
        P("grid", None),
        P(),
        P("grid"),
        P(),
        P(),
        P("grid", None),
        P("grid", None),
    )
    out_specs = (
        P(None, ("member", "grid")),
        P(None, ("member", "grid")),
        P(("member", "grid"), None),
        P(None, ("member", "grid")),
        P(("member", "grid"), None),
    )
    return jax.shard_map(
        per_device, mesh=mesh, in_specs=in_specs, out_specs=out_specs, check_vma=False
    )
```

profile of v0, /device:TPU:8, one launch (start us, length us, event | category | flops | bytes accessed | tf_op | source)
XLA Modules:
  0.0 715.8 jit_solution(16894193995473229864)
XLA Ops:
  16.0 158.6 %all-reduce.9.cloned.1.call-done = bf16[256,256]{1,0:T(8,128)(2,1)} async-done(((bf16[256,256]{1,0:T(8,128)(2,1)}), bf16[256,256]{1,0:T(8,128)(2,1)}) %all-reduce.9.cloned.1.call-update) | async-done | bytes 131088 | tf_op jit(solution)/shard_map/psum | solution.py:30
  178.8 3.3 multiply_convert_fusion
  184.5 3.1 gather_fusion.1
  187.6 3.1 gather_fusion.2
  196.9 3.1 gather_fusion.5
  200.0 3.1 gather_fusion.6
  214.9 3.8 collective-permute-done.2
  232.4 3.6 gather_fusion.8
  236.0 3.5 gather_fusion.9
  239.5 3.5 gather_fusion.10
  245.9 6.5 all-to-all-start
  253.2 7.8 %all-to-all-done = bf16[16,16,128]{2,1,0:T(8,128)(2,1)} async-done(((bf16[16,16,128]{2,1,0:T(8,128)(2,1)}), bf16[16,16,128]{2,1,0:T(8,128)(2,1)}, u32[]{:S(2)}, u32[]{:S(2)}) %all-to-all-start) | async-done | bytes 65568 | tf_op jit(solution)/shard_map/all_to_all | solution.py:68
  263.7 4.1 all-to-all-start.1
  270.2 6.1 all-to-all-done.1
  278.5 4.6 scatter_custom_fusion
  283.2 5.6 scatter_custom_fusion.1
  288.8 5.6 scatter_custom_fusion.2
  295.8 5.6 collective-permute-start.6
  317.0 6.5 collective-permute-start.8
  323.5 6.2 collective-permute-start.9
  341.3 3.4 scatter-add.106
  349.1 3.7 fusion.87
  356.1 3.7 scatter_custom_fusion.3
  359.8 5.1 scatter_custom_fusion.4
  364.9 5.1 scatter_custom_fusion.5
  370.1 5.1 scatter_custom_fusion.6
  375.2 5.1 scatter_custom_fusion.7
  380.3 5.1 scatter_custom_fusion.8
  385.4 5.3 scatter_custom_fusion.9
  390.8 5.1 scatter_custom_fusion.10
  395.9 5.2 fusion.3
  401.1 301.0 %all-reduce.11.cloned.1.call-done = (f32[16,1024]{1,0:T(8,128)}, f32[128,1024]{0,1:T(8,128)}, f32[1024,1536]{1,0:T(8,128)}, f32[512,1024]{0,1:T(8,128)}, f32[1024,128]{1,0:T(8,128)}) async-done(((f32[16,1024]{1,0:T(8,128)}, f32[128,1024]{0,1:T(8,128)}, f32[1024,1536]{1,0:T(8,128)}, f32[512,1024]{0,1:T(8,128)}, f32[1024,128]{1,0:T(8,128)}), (f32[16,1024]{1,0:T(8,128)}, f32[128,1024]{0,1:T(8,128)}, ...) | async-done | bytes 9502736
  (263 shorter events, 99.6 us)
Async XLA Ops:
  7.2 202.7 %copy-start = (bf16[1024,1536]{1,0:T(8,128)(2,1)S(1)}, bf16[1024,1536]{1,0:T(8,128)(2,1)}, u32[]{:S(2)}) copy-start(bf16[1024,1536]{1,0:T(8,128)(2,1)} %param.32) | copy-start | bytes 9437188
  7.2 167.5 %all-reduce.9.cloned.1.call-start = ((), (), s32[]{:S(2)}) async-start(), calls=%async_computation.2 | async-start | bytes 262144 | tf_op jit(solution)/shard_map/psum | solution.py:30
  9.5 172.6 %copy-start.58 = (s32[128]{0:T(128)}, s32[128]{0:T(128)S(1)}, u32[]{:S(2)}) copy-start(s32[128]{0:T(128)S(1)} %get-tuple-element.141) | copy-start | bytes 1540
  10.5 195.7 %copy-start.31 = (f32[128]{0:T(128)}, f32[128]{0:T(128)S(1)}, u32[]{:S(2)}) copy-start(f32[128]{0:T(128)S(1)} %get-tuple-element.132) | copy-start | bytes 1540
  10.5 195.7 %copy-start.33 = (f32[128]{0:T(128)}, f32[128]{0:T(128)S(1)}, u32[]{:S(2)}) copy-start(f32[128]{0:T(128)S(1)} %get-tuple-element.138) | copy-start | bytes 1540
  10.6 195.7 %copy-start.35 = (f32[128]{0:T(128)}, f32[128]{0:T(128)S(1)}, u32[]{:S(2)}) copy-start(f32[128]{0:T(128)S(1)} %get-tuple-element.139) | copy-start | bytes 1540
  10.6 195.7 %copy-start.37 = (f32[128]{0:T(128)}, f32[128]{0:T(128)S(1)}, u32[]{:S(2)}) copy-start(f32[128]{0:T(128)S(1)} %get-tuple-element.133) | copy-start | bytes 1540
  10.6 195.7 %copy-start.39 = (f32[128]{0:T(128)}, f32[128]{0:T(128)S(1)}, u32[]{:S(2)}) copy-start(f32[128]{0:T(128)S(1)} %get-tuple-element.134) | copy-start | bytes 1540
  10.6 195.7 %copy-start.41 = (f32[128]{0:T(128)}, f32[128]{0:T(128)S(1)}, u32[]{:S(2)}) copy-start(f32[128]{0:T(128)S(1)} %get-tuple-element.135) | copy-start | bytes 1540
  10.6 195.7 %copy-start.43 = (f32[128]{0:T(128)}, f32[128]{0:T(128)S(1)}, u32[]{:S(2)}) copy-start(f32[128]{0:T(128)S(1)} %get-tuple-element.136) | copy-start | bytes 1540
  10.6 195.7 %copy-start.45 = (f32[128]{0:T(128)}, f32[128]{0:T(128)S(1)}, u32[]{:S(2)}) copy-start(f32[128]{0:T(128)S(1)} %get-tuple-element.137) | copy-start | bytes 1540
  175.4 3.3 collective-permute-start
  175.4 3.3 collective-permute-start.1
  212.8 5.9 collective-permute-start.2
  214.5 4.3 collective-permute-start.3
  219.9 48.1 %copy-start.14 = (bf16[256,512]{0,1:T(8,128)(2,1)}, bf16[256,512]{0,1:T(8,128)(2,1)S(1)}, u32[]{:S(2)}) copy-start(bf16[256,512]{0,1:T(8,128)(2,1)S(1)} %get-tuple-element.111) | copy-start | bytes 786436
  226.7 4.9 collective-permute-start.4
  228.5 3.1 collective-permute-start.5
  245.9 15.0 %all-to-all-start = ((bf16[16,16,128]{2,1,0:T(8,128)(2,1)}), bf16[16,16,128]{2,1,0:T(8,128)(2,1)}, u32[]{:S(2)}, u32[]{:S(2)}) async-start(bf16[16,16,128]{2,1,0:T(8,128)(2,1)} %bitcast.159), calls=%async_computation | async-start | bytes 131072 | tf_op jit(solution)/shard_map/all_to_all | solution.py:68
  263.7 12.6 %all-to-all-start.1 = ((bf16[16,16,128]{2,1,0:T(8,128)(2,1)}), bf16[16,16,128]{2,1,0:T(8,128)(2,1)}, u32[]{:S(2)}, u32[]{:S(2)}) async-start(bf16[16,16,128]{2,1,0:T(8,128)(2,1)} %multiply_convert_fusion.4), calls=%async_computation.1 | async-start | bytes 131072 | tf_op jit(solution)/shard_map/all_to_all | solution.py:68
  267.9 10.7 %copy-start.48 = (f32[256,1]{0,1:T(1,128)S(1)}, f32[256,1]{0,1:T(1,128)}, u32[]{:S(2)}) copy-start(f32[256,1]{0,1:T(1,128)} %get-tuple-element.126) | copy-start | bytes 3076
  267.9 434.2 %all-reduce.11.cloned.1.call-start = ((), (), s32[]{:S(2)}) async-start(), calls=%async_computation.3 | async-start | bytes 19005440
  270.1 13.0 %copy-start.50 = (f32[256,1]{0,1:T(1,128)S(1)}, f32[256,1]{0,1:T(1,128)}, u32[]{:S(2)}) copy-start(f32[256,1]{0,1:T(1,128)} %get-tuple-element.128) | copy-start | bytes 3076
  294.3 11.0 %copy-start.10 = (f32[256,1024]{1,0:T(8,128)S(1)}, f32[256,1024]{1,0:T(8,128)}, u32[]{:S(2)}) copy-start(f32[256,1024]{1,0:T(8,128)} %scatter_custom_fusion.2) | copy-start | bytes 3145732
  295.8 9.6 %collective-permute-start.6 = (bf16[64,1024]{1,0:T(8,128)(2,1)S(1)}, bf16[64,1024]{1,0:T(8,128)(2,1)S(1)}, u32[]{:S(2)}, u32[]{:S(2)}) collective-permute-start(bf16[64,1024]{1,0:T(8,128)(2,1)S(1)} %get-tuple-element.109), channel_id=1, source_target_pairs={{0,1},{1,2},{2,3},{3,4},{4,5},{5,6},{6,7},{7,8},{8,9},{9,10},{10,1... | collective-permute-start | bytes 393224 | tf_op jit(solution)/shard_map/ppermute | solution.py:20
  301.4 4.0 collective-permute-start.7
  316.0 13.7 %copy-start.15 = (bf16[256,512]{0,1:T(8,128)(2,1)S(1)}, bf16[256,512]{0,1:T(8,128)(2,1)}, u32[]{:S(2)}) copy-start(bf16[256,512]{0,1:T(8,128)(2,1)} %copy-done.14) | copy-start | bytes 786436
  317.0 16.2 %collective-permute-start.8 = (bf16[64,1024]{0,1:T(8,128)(2,1)S(1)}, bf16[64,1024]{0,1:T(8,128)(2,1)S(1)}, u32[]{:S(2)}, u32[]{:S(2)}) collective-permute-start(bf16[64,1024]{0,1:T(8,128)(2,1)S(1)} %get-tuple-element.107), channel_id=1, source_target_pairs={{0,1},{1,2},{2,3},{3,4},{4,5},{5,6},{6,7},{7,8},{8,9},{9,10},{10,1... | collective-permute-start | bytes 393224 | tf_op jit(solution)/shard_map/ppermute | solution.py:20
  323.5 10.1 %collective-permute-start.9 = (bf16[64,1024]{0,1:T(8,128)(2,1)S(1)}, bf16[64,1024]{0,1:T(8,128)(2,1)S(1)}, u32[]{:S(2)}, u32[]{:S(2)}) collective-permute-start(bf16[64,1024]{0,1:T(8,128)(2,1)S(1)} %get-tuple-element.108), channel_id=1, source_target_pairs={{1,0},{2,1},{3,2},{4,3},{5,4},{6,5},{7,6},{8,7},{9,8},{10,9},{11,1... | collective-permute-start | bytes 393224 | tf_op jit(solution)/shard_map/ppermute | solution.py:23
  385.4 10.5 %copy-start.23 = (bf16[256,128]{1,0:T(8,128)(2,1)S(1)}, bf16[256,128]{1,0:T(8,128)(2,1)}, u32[]{:S(2)}) copy-start(bf16[256,128]{1,0:T(8,128)(2,1)} %copy-done.22) | copy-start | bytes 196612
  385.4 10.5 %copy-start.70 = (bf16[128,128]{1,0:T(8,128)(2,1)S(1)}, bf16[128,128]{1,0:T(8,128)(2,1)}, u32[]{:S(2)}) copy-start(bf16[128,128]{1,0:T(8,128)(2,1)} %copy-done.69) | copy-start | bytes 98308
  385.4 10.5 %copy-start.72 = (bf16[128,128]{1,0:T(8,128)(2,1)S(1)}, bf16[128,128]{1,0:T(8,128)(2,1)}, u32[]{:S(2)}) copy-start(bf16[128,128]{1,0:T(8,128)(2,1)} %copy-done.71) | copy-start | bytes 98308
  (55 other events, 260.0 us)
Sparse Core Ops, SparseCore 0:
  10.6 164.0 all-reduce.8
  401.3 300.7 all-reduce.10
where the time goes:
time: 727 us; the launch traced here: 716 us
  waiting for transfers between devices  483 us (66%)
  other arithmetic  82 us (11%)
  local copies, waits for them, and re-layouts  59.2 us (8%)
  matrix products  40.1 us (6%)
  starting transfers between devices  36.1 us (5%)
  between operations  15.9 us (2%)
    unnamed x3, waiting for transfers between devices  301 us
    psum x1, waiting for transfers between devices, broadcast(): return lax.psum(jnp.where(mine, x, jnp.zeros_like(x)), axis)  159 us
    scatter-add x8, other arithmetic, per_device(): grad_messages.at[enc_source[:, arc_location]]  39.7 us
    gather x8, local copies, waits for them, and re-layouts, per_device(): messages[enc_source[:, arc_location]].astype(jnp.float32)  24.1 us
    scatter-add x3, other arithmetic, per_device(): grad_dnorm_ext.at[unpacker_start_cell[:, arc_location]]  15.8 us
    ppermute x5, starting transfers between devices, extended(): lax.ppermute(lax.slice_in_dim(block, block.shape[dim] - width, None, axis...  15.6 us
  transfers between devices with their start and end apart: 14, of which 10 were waited for; matrix products, arithmetic and copies ran while one was open for 2% of the time, Pallas kernels for 0%

commit v1 on v0

--- a/solution.py
+++ b/solution.py
@@ -27,7 +27,7 @@
 
 def broadcast(x, axis, root):
     mine = lax.axis_index(axis) == root
-    return lax.psum(jnp.where(mine, x, jnp.zeros_like(x)), axis)
+    return jnp.sum(lax.all_gather(jnp.where(mine, x, jnp.zeros_like(x)), axis), axis=0)
 
 
 def rms_factor(values):

time: 727 us -> 649 us (0.89)
  waiting for transfers between devices: 483 us -> 404 us
    psum x1 -> x0, waiting for transfers between devices: 159 us -> none  [broadcast(): return lax.psum(jnp.where(mine, x, jnp.zeros_like(x)), axis)]
    all_gather x0 -> x1, waiting for transfers between devices: none -> 78.9 us  [broadcast(): lax.all_gather(jnp.where(mine, x, jnp.zeros_like(x)), axis)]
where the time goes in v1:
time: 649 us; the launch traced here: 638 us
  waiting for transfers between devices  404 us (62%)
  other arithmetic  83.9 us (13%)
  local copies, waits for them, and re-layouts  57.9 us (9%)
  matrix products  40.1 us (6%)
  starting transfers between devices  36.2 us (6%)
  between operations  15.9 us (2%)
    unnamed x3, waiting for transfers between devices  301 us
    all_gather x1, waiting for transfers between devices, broadcast(): lax.all_gather(jnp.where(mine, x, jnp.zeros_like(x)), axis)  78.9 us
    scatter-add x8, other arithmetic, per_device(): grad_messages.at[enc_source[:, arc_location]]  39.7 us
    gather x8, local copies, waits for them, and re-layouts, per_device(): messages[enc_source[:, arc_location]].astype(jnp.float32)  24.1 us
    ppermute x5, starting transfers between devices, extended(): lax.ppermute(lax.slice_in_dim(block, block.shape[dim] - width, None, axis...  15.9 us
    scatter-add x3, other arithmetic, per_device(): grad_dnorm_ext.at[unpacker_start_cell[:, arc_location]]  15.8 us
    all_to_all x2, waiting for transfers between devices, realization_rotate(): lax.all_to_all(values.astype(jnp.bfloat16), 'member', split_axis=0, conca...  13.9 us
  transfers between devices with their start and end apart: 14, of which 10 were waited for; matrix products, arithmetic and copies ran while one was open for 2% of the time, Pallas kernels for 0%

profile of v1, /device:TPU:8, one launch (start us, length us, event | category | flops | bytes accessed | tf_op | source)
XLA Modules:
  0.0 637.7 jit_solution(4973830997766377873)
XLA Ops:
  16.5 78.9 %all-gather.2.cloned.1.call-done = bf16[16,256,256]{2,1,0:T(8,128)(2,1)} async-done(((bf16[1,256,256]{2,1,0:T(8,128)(2,1)}), bf16[16,256,256]{2,1,0:T(8,128)(2,1)}) %all-gather.2.cloned.1.call-update) | async-done | bytes 2097168 | tf_op jit(solution)/shard_map/all_gather | solution.py:30
  100.8 3.3 multiply_convert_fusion
  106.6 3.1 gather_fusion.1
  109.7 3.1 gather_fusion.2
  112.8 3.1 gather_fusion.3
  122.1 3.1 gather_fusion.6
  136.9 3.8 collective-permute-done.2
  154.4 3.6 gather_fusion.8
  158.0 3.5 gather_fusion.9
  161.4 3.5 gather_fusion.10
  167.8 6.5 %all-to-all-start = ((bf16[16,16,128]{2,1,0:T(8,128)(2,1)}), bf16[16,16,128]{2,1,0:T(8,128)(2,1)}, u32[]{:S(2)}, u32[]{:S(2)}) async-start(bf16[16,16,128]{2,1,0:T(8,128)(2,1)} %bitcast.157), calls=%async_computation | async-start | bytes 131072 | tf_op jit(solution)/shard_map/all_to_all | solution.py:68
  175.1 7.8 %all-to-all-done = bf16[16,16,128]{2,1,0:T(8,128)(2,1)} async-done(((bf16[16,16,128]{2,1,0:T(8,128)(2,1)}), bf16[16,16,128]{2,1,0:T(8,128)(2,1)}, u32[]{:S(2)}, u32[]{:S(2)}) %all-to-all-start) | async-done | bytes 65568 | tf_op jit(solution)/shard_map/all_to_all | solution.py:68
  185.6 4.1 all-to-all-start.1
  192.1 6.1 all-to-all-done.1
  200.5 4.6 scatter_custom_fusion
  205.1 5.6 scatter_custom_fusion.1
  210.7 5.6 scatter_custom_fusion.2
  217.7 5.7 collective-permute-start.6
  238.9 6.6 %collective-permute-start.8 = (bf16[64,1024]{0,1:T(8,128)(2,1)S(1)}, bf16[64,1024]{0,1:T(8,128)(2,1)S(1)}, u32[]{:S(2)}, u32[]{:S(2)}) collective-permute-start(bf16[64,1024]{0,1:T(8,128)(2,1)S(1)} %get-tuple-element.107), channel_id=1, source_target_pairs={{0,1},{1,2},{2,3},{3,4},{4,5},{5,6},{6,7},{7,8},{8,9},{9,10},{10,1... | collective-permute-start | bytes 393224 | tf_op jit(solution)/shard_map/ppermute | solution.py:20
  245.5 6.0 collective-permute-start.9
  263.2 3.4 scatter-add.106
  271.0 3.7 fusion.87
  278.0 3.7 scatter_custom_fusion.3
  281.7 5.1 scatter_custom_fusion.4
  286.8 5.1 scatter_custom_fusion.5
  291.9 5.1 scatter_custom_fusion.6
  297.0 5.1 scatter_custom_fusion.7
  302.2 5.1 scatter_custom_fusion.8
  307.3 5.3 scatter_custom_fusion.9
  312.6 5.1 scatter_custom_fusion.10
  317.8 5.2 fusion.3
  323.0 301.0 %all-reduce.8.cloned.1.call-done = (f32[16,1024]{1,0:T(8,128)}, f32[128,1024]{0,1:T(8,128)}, f32[1024,1536]{1,0:T(8,128)}, f32[512,1024]{0,1:T(8,128)}, f32[1024,128]{1,0:T(8,128)}) async-done(((f32[16,1024]{1,0:T(8,128)}, f32[128,1024]{0,1:T(8,128)}, f32[1024,1536]{1,0:T(8,128)}, f32[512,1024]{0,1:T(8,128)}, f32[1024,128]{1,0:T(8,128)}), (f32[16,1024]{1,0:T(8,128)}, f32[128,1024]{0,1:T(8,128)}, ...) | async-done | bytes 9502736
  (266 shorter events, 101.1 us)
Async XLA Ops:
  7.2 124.7 %copy-start = (bf16[1024,1536]{1,0:T(8,128)(2,1)S(1)}, bf16[1024,1536]{1,0:T(8,128)(2,1)}, u32[]{:S(2)}) copy-start(bf16[1024,1536]{1,0:T(8,128)(2,1)} %param.32) | copy-start | bytes 9437188
  7.2 88.3 %all-gather.2.cloned.1.call-start = ((), (), s32[]{:S(2)}) async-start(), calls=%async_computation.2 | async-start | bytes 2228224 | tf_op jit(solution)/shard_map/all_gather | solution.py:30
  11.4 92.7 %copy-start.59 = (s32[128]{0:T(128)}, s32[128]{0:T(128)S(1)}, u32[]{:S(2)}) copy-start(s32[128]{0:T(128)S(1)} %get-tuple-element.141) | copy-start | bytes 1540
  15.0 113.3 %copy-start.32 = (f32[128]{0:T(128)}, f32[128]{0:T(128)S(1)}, u32[]{:S(2)}) copy-start(f32[128]{0:T(128)S(1)} %get-tuple-element.132) | copy-start | bytes 1540
  15.0 113.3 %copy-start.34 = (f32[128]{0:T(128)}, f32[128]{0:T(128)S(1)}, u32[]{:S(2)}) copy-start(f32[128]{0:T(128)S(1)} %get-tuple-element.138) | copy-start | bytes 1540
  15.0 113.3 %copy-start.36 = (f32[128]{0:T(128)}, f32[128]{0:T(128)S(1)}, u32[]{:S(2)}) copy-start(f32[128]{0:T(128)S(1)} %get-tuple-element.139) | copy-start | bytes 1540
  15.0 113.2 %copy-start.38 = (f32[128]{0:T(128)}, f32[128]{0:T(128)S(1)}, u32[]{:S(2)}) copy-start(f32[128]{0:T(128)S(1)} %get-tuple-element.133) | copy-start | bytes 1540
  15.1 113.2 %copy-start.40 = (f32[128]{0:T(128)}, f32[128]{0:T(128)S(1)}, u32[]{:S(2)}) copy-start(f32[128]{0:T(128)S(1)} %get-tuple-element.134) | copy-start | bytes 1540
  15.1 113.2 %copy-start.42 = (f32[128]{0:T(128)}, f32[128]{0:T(128)S(1)}, u32[]{:S(2)}) copy-start(f32[128]{0:T(128)S(1)} %get-tuple-element.135) | copy-start | bytes 1540
  15.1 113.2 %copy-start.44 = (f32[128]{0:T(128)}, f32[128]{0:T(128)S(1)}, u32[]{:S(2)}) copy-start(f32[128]{0:T(128)S(1)} %get-tuple-element.136) | copy-start | bytes 1540
  15.1 113.2 %copy-start.46 = (f32[128]{0:T(128)}, f32[128]{0:T(128)S(1)}, u32[]{:S(2)}) copy-start(f32[128]{0:T(128)S(1)} %get-tuple-element.137) | copy-start | bytes 1540
  97.4 3.4 collective-permute-start
  97.4 3.3 collective-permute-start.1
  134.8 5.9 collective-permute-start.2
  136.4 4.3 collective-permute-start.3
  141.8 48.1 %copy-start.14 = (bf16[256,512]{0,1:T(8,128)(2,1)}, bf16[256,512]{0,1:T(8,128)(2,1)S(1)}, u32[]{:S(2)}) copy-start(bf16[256,512]{0,1:T(8,128)(2,1)S(1)} %get-tuple-element.111) | copy-start | bytes 786436
  148.6 4.9 collective-permute-start.4
  150.4 3.1 collective-permute-start.5
  167.8 15.0 %all-to-all-start = ((bf16[16,16,128]{2,1,0:T(8,128)(2,1)}), bf16[16,16,128]{2,1,0:T(8,128)(2,1)}, u32[]{:S(2)}, u32[]{:S(2)}) async-start(bf16[16,16,128]{2,1,0:T(8,128)(2,1)} %bitcast.157), calls=%async_computation | async-start | bytes 131072 | tf_op jit(solution)/shard_map/all_to_all | solution.py:68
  185.6 12.6 %all-to-all-start.1 = ((bf16[16,16,128]{2,1,0:T(8,128)(2,1)}), bf16[16,16,128]{2,1,0:T(8,128)(2,1)}, u32[]{:S(2)}, u32[]{:S(2)}) async-start(bf16[16,16,128]{2,1,0:T(8,128)(2,1)} %multiply_convert_fusion.4), calls=%async_computation.1 | async-start | bytes 131072 | tf_op jit(solution)/shard_map/all_to_all | solution.py:68
  189.8 10.7 %copy-start.49 = (f32[256,1]{0,1:T(1,128)S(1)}, f32[256,1]{0,1:T(1,128)}, u32[]{:S(2)}) copy-start(f32[256,1]{0,1:T(1,128)} %get-tuple-element.126) | copy-start | bytes 3076
  189.8 434.2 %all-reduce.8.cloned.1.call-start = ((), (), s32[]{:S(2)}) async-start(), calls=%async_computation.3 | async-start | bytes 19005440
  192.1 13.0 %copy-start.51 = (f32[256,1]{0,1:T(1,128)S(1)}, f32[256,1]{0,1:T(1,128)}, u32[]{:S(2)}) copy-start(f32[256,1]{0,1:T(1,128)} %get-tuple-element.128) | copy-start | bytes 3076
  216.3 11.0 %copy-start.10 = (f32[256,1024]{1,0:T(8,128)S(1)}, f32[256,1024]{1,0:T(8,128)}, u32[]{:S(2)}) copy-start(f32[256,1024]{1,0:T(8,128)} %scatter_custom_fusion.2) | copy-start | bytes 3145732
  217.7 9.6 %collective-permute-start.6 = (bf16[64,1024]{1,0:T(8,128)(2,1)S(1)}, bf16[64,1024]{1,0:T(8,128)(2,1)S(1)}, u32[]{:S(2)}, u32[]{:S(2)}) collective-permute-start(bf16[64,1024]{1,0:T(8,128)(2,1)S(1)} %get-tuple-element.109), channel_id=1, source_target_pairs={{0,1},{1,2},{2,3},{3,4},{4,5},{5,6},{6,7},{7,8},{8,9},{9,10},{10,1... | collective-permute-start | bytes 393224 | tf_op jit(solution)/shard_map/ppermute | solution.py:20
  223.4 3.9 collective-permute-start.7
  237.9 13.7 %copy-start.15 = (bf16[256,512]{0,1:T(8,128)(2,1)S(1)}, bf16[256,512]{0,1:T(8,128)(2,1)}, u32[]{:S(2)}) copy-start(bf16[256,512]{0,1:T(8,128)(2,1)} %copy-done.14) | copy-start | bytes 786436
  238.9 16.2 %collective-permute-start.8 = (bf16[64,1024]{0,1:T(8,128)(2,1)S(1)}, bf16[64,1024]{0,1:T(8,128)(2,1)S(1)}, u32[]{:S(2)}, u32[]{:S(2)}) collective-permute-start(bf16[64,1024]{0,1:T(8,128)(2,1)S(1)} %get-tuple-element.107), channel_id=1, source_target_pairs={{0,1},{1,2},{2,3},{3,4},{4,5},{5,6},{6,7},{7,8},{8,9},{9,10},{10,1... | collective-permute-start | bytes 393224 | tf_op jit(solution)/shard_map/ppermute | solution.py:20
  245.5 9.9 %collective-permute-start.9 = (bf16[64,1024]{0,1:T(8,128)(2,1)S(1)}, bf16[64,1024]{0,1:T(8,128)(2,1)S(1)}, u32[]{:S(2)}, u32[]{:S(2)}) collective-permute-start(bf16[64,1024]{0,1:T(8,128)(2,1)S(1)} %get-tuple-element.108), channel_id=1, source_target_pairs={{1,0},{2,1},{3,2},{4,3},{5,4},{6,5},{7,6},{8,7},{9,8},{10,9},{11,1... | collective-permute-start | bytes 393224 | tf_op jit(solution)/shard_map/ppermute | solution.py:23
  307.3 10.5 %copy-start.24 = (bf16[256,128]{1,0:T(8,128)(2,1)S(1)}, bf16[256,128]{1,0:T(8,128)(2,1)}, u32[]{:S(2)}) copy-start(bf16[256,128]{1,0:T(8,128)(2,1)} %copy-done.23) | copy-start | bytes 196612
  307.3 10.5 %copy-start.71 = (bf16[128,128]{1,0:T(8,128)(2,1)S(1)}, bf16[128,128]{1,0:T(8,128)(2,1)}, u32[]{:S(2)}) copy-start(bf16[128,128]{1,0:T(8,128)(2,1)} %copy-done.70) | copy-start | bytes 98308
  307.3 10.5 %copy-start.73 = (bf16[128,128]{1,0:T(8,128)(2,1)S(1)}, bf16[128,128]{1,0:T(8,128)(2,1)}, u32[]{:S(2)}) copy-start(bf16[128,128]{1,0:T(8,128)(2,1)} %copy-done.72) | copy-start | bytes 98308
  (56 other events, 233.2 us)
Sparse Core Ops, SparseCore 0:
  9.8 85.6 all-gather.1
  323.1 300.8 all-reduce.7
